TPU v7x, 1024 devices: a whole 4x4x32 slice. The times are simulated.
1024 devices in a mesh: row: 32 (over z), col: 32 (over y, x, core).
Axes of the slice: x: 4, y: 4, z: 32, core: 2. Of those that a mesh axis runs over, the one named last changes fastest.
Arguments:
- volume: float32 [32, 32, 8, 24, 256], P('row', 'col'), may hold values from 0 to 2
- blocks_across: bfloat16 [32, 256, 256], replicated, may hold values from -0.375 to 0.375
- downward_ray_blocks: bfloat16 [32, 256, 256], replicated, may hold values from -0.375 to 0.375
- tiles_across: int32 [32, 32, 32], P('row', 'col'), may hold values from 0 to 7
- tiles_down: int32 [32, 32, 32], P('row', 'col'), may hold values from 0 to 7
- footprint_across: int32 [32, 32, 32], P('row', 'col'), may hold values from 64 to 256
- footprint_down: int32 [32, 32, 32], P('row', 'col'), may hold values from 64 to 256
- rays_across: int32 [32, 32, 32], P('row', 'col'), may hold values from 0 to 63, as said below
- rays_down: int32 [32, 32, 32], P('row', 'col'), may hold values from 0 to 63, as said below
- owners_across: int32 [32, 64], P('row'), may hold values from 0 to 63, as said below
- owners_down: int32 [32, 64], P('col'), may hold values from 0 to 63, as said below
- observed_sinogram_across: float32 [32, 32, 2, 24, 256], P('row', 'col'), may hold values from -24 to 24
- observed_sinogram_down: float32 [32, 32, 2, 24, 256], P('row', 'col'), may hold values from -24 to 24
- weights_across: float32 [32, 32, 2, 24, 256], P('row', 'col'), may hold values from 0.25 to 1
- weights_down: float32 [32, 32, 2, 24, 256], P('row', 'col'), may hold values from 0.25 to 1
Outputs:
- volume_out: float32 [32, 32, 8, 24, 256], P('row', 'col')
- residual_across: float32 [32, 32, 2, 24, 256], P('row', 'col')
- residual_down: float32 [32, 32, 2, 24, 256], P('row', 'col')
Inputs may be any that keep to these rules, and one draw needn't show every extreme that they name: `rays_across`: ray ids are numbered within the device's row group. On one device no ray id appears twice, no owner column (owners_across[i, ray] // 2) is named by more than 2 slots, and on every device some owner column is named by exactly 2. `rays_down`: ray ids are numbered within the device's column group. On one device no ray id appears twice, no owner row (owners_down[j, ray] // 2) is named by more than 2 slots, and on every device some owner row is named by exactly 2. `owners_across`: each row is a permutation of 0 to 63. `owners_down`: each row is a permutation of 0 to 63.
All inputs are finite; a program needn't handle non-finite values.
Results may differ from a plain program's by a relative error of at most 0.028.
Values may be sent and summed in bfloat16 or wider, within the bound.
A program may use at most 32 MiB of HBM per device.

v0:
```python
import jax
import jax.numpy as jnp
from jax import lax
from jax.sharding import PartitionSpec as P

OWNED = 2
CAP = 2
ITERS = 2


HUBER_DELTA = 0.5
STEP_SIZE = 0.05
SMOOTH_WEIGHT = 1.0


def route_tables(ray_list, owner_row, per_owner, capacity, peers):
    group_member_count = owner_row.shape[0]
    matches = ray_list[:, None] == jnp.arange(group_member_count, dtype=jnp.int32)[None, :]
    position = jnp.sum(jnp.where(matches, owner_row[None, :], 0), axis=1)
    target = position // per_owner
    local_index = position % per_owner
    num_items = ray_list.shape[0]
    earlier = jnp.arange(num_items)[None, :] < jnp.arange(num_items)[:, None]
    ranking = jnp.sum((target[:, None] == target[None, :]) & earlier, axis=1)
    slot_index = target * capacity + ranking
    placing = slot_index[None, :] == jnp.arange(peers * capacity, dtype=jnp.int32)[:, None]
    slot_local = jnp.sum(jnp.where(placing, local_index[None, :] + 1, 0), axis=1) - 1
    return (position, placing.astype(jnp.bfloat16), slot_local)


def project(volume_bf, blocks, tiles, ray_mask):
    chosen = jnp.take(volume_bf, tiles, axis=0)
    partial_value = jnp.einsum("svt,str->svr", chosen, blocks, preferred_element_type=jnp.float32)
    return jnp.where(ray_mask[:, None, :], partial_value, 0.0).astype(jnp.bfloat16)


def back_project(items, blocks, tile_pick, ray_mask):
    masked = jnp.where(ray_mask[:, None, :], items, jnp.zeros_like(items))
    contrib = jnp.einsum("svr,str->svt", masked, blocks, preferred_element_type=jnp.float32)
    return jnp.einsum("sk,svt->kvt", tile_pick, contrib, precision=lax.Precision.HIGHEST)


def smooth_gradient(voxels):
    diff = voxels[..., 1:, :] - voxels[..., :-1, :]
    slope = jnp.clip(diff, -HUBER_DELTA, HUBER_DELTA)
    zero_row = jnp.zeros_like(slope[..., :1, :])
    return jnp.concatenate([zero_row, slope], axis=-2) - jnp.concatenate([slope, zero_row], axis=-2)


def dense_route(partial_value, position, measured, weights, reduce_rows, spread_rows):

    def ray_term(first_row, num_rows):
        wanted = (position[None, :] == jnp.arange(num_rows, dtype=jnp.int32)[:, None]).astype(
            jnp.bfloat16
        )
        return jnp.einsum("ks,svr->kvr", wanted, partial_value, preferred_element_type=jnp.float32)

    projection = reduce_rows(ray_term, measured.shape[0])
    residual = weights * (measured - projection)

    def collect(total_sum, received, first_row):
        wanted = (
            position[:, None] == jnp.arange(received.shape[0], dtype=jnp.int32)[None, :]
        ).astype(jnp.bfloat16)
        return jnp.einsum("sk,kvr->svr", wanted, received, preferred_element_type=jnp.float32)

    empty_sum = jnp.zeros(partial_value.shape, jnp.float32)
    items = spread_rows(residual.astype(jnp.bfloat16), collect, empty_sum).astype(jnp.bfloat16)
    return (residual, items)


def shards(
    volume,
    blocks_across,
    downward_ray_blocks,
    tiles_across,
    tiles_down,
    footprint_across,
    footprint_down,
    rays_across,
    rays_down,
    owners_across,
    owners_down,
    observed_sinogram_across,
    observed_sinogram_down,
    weights_across,
    weights_down,
):
    voxels = volume[0, 0]
    num_tiles = voxels.shape[0]
    ray_count = blocks_across.shape[2]
    ray_index = jnp.arange(ray_count, dtype=jnp.int32)
    tile_index = jnp.arange(num_tiles, dtype=jnp.int32)
    pos_across, place_across, local_across = route_tables(
        rays_across[0, 0], owners_across[0], OWNED, CAP, lax.axis_size("col")
    )
    pos_down, place_down, local_down = route_tables(
        rays_down[0, 0], owners_down[0], OWNED, CAP, lax.axis_size("row")
    )
    mask_across = ray_index[None, :] < footprint_across[0, 0][:, None]
    mask_down = ray_index[None, :] < footprint_down[0, 0][:, None]
    pick_across = (tiles_across[0, 0][:, None] == tile_index[None, :]).astype(jnp.float32)
    pick_down = (tiles_down[0, 0][:, None] == tile_index[None, :]).astype(jnp.float32)
    measurement_across_rows = observed_sinogram_across[0, 0]
    measurement_down_rows = observed_sinogram_down[0, 0]
    weight_across = weights_across[0, 0]
    weight_down = weights_down[0, 0]
    misfit_across_rays = measurement_across_rows
    misfit_down_rays = measurement_down_rows
    for iteration in range(ITERS):
        volume_bf = voxels.astype(jnp.bfloat16)
        part_across = project(volume_bf, blocks_across, tiles_across[0, 0], mask_across)
        part_down = project(volume_bf, downward_ray_blocks, tiles_down[0, 0], mask_down)
        misfit_across_rays, items_across = dense_route(
            part_across,
            pos_across,
            measurement_across_rows,
            weight_across,
            lambda term_fn, num_rows: lax.psum_scatter(
                term_fn(jnp.int32(0), num_rows * lax.axis_size("col")).astype(jnp.bfloat16),
                "col",
                scatter_dimension=0,
                tiled=True,
            ).astype(jnp.float32),
            lambda values, fold_fn, initial: fold_fn(
                initial, lax.all_gather(values, "col", axis=0, tiled=True), jnp.int32(0)
            ),
        )
        misfit_down_rays, items_down = dense_route(
            part_down,
            pos_down,
            measurement_down_rows,
            weight_down,
            lambda term_fn, num_rows: lax.psum_scatter(
                term_fn(jnp.int32(0), num_rows * lax.axis_size("row")).astype(jnp.bfloat16),
                "row",
                scatter_dimension=0,
                tiled=True,
            ).astype(jnp.float32),
            lambda values, fold_fn, initial: fold_fn(
                initial, lax.all_gather(values, "row", axis=0, tiled=True), jnp.int32(0)
            ),
        )
        gradient = back_project(items_across, blocks_across, pick_across, mask_across)
        gradient = gradient + back_project(items_down, downward_ray_blocks, pick_down, mask_down)
        voxels = jnp.maximum(
            voxels + STEP_SIZE * (gradient - SMOOTH_WEIGHT * smooth_gradient(voxels)), 0.0
        )
    return (voxels[None, None], misfit_across_rays[None, None], misfit_down_rays[None, None])


def solution(mesh):
    return jax.shard_map(
        shards,
        mesh=mesh,
        in_specs=(
            P("row", "col", None, None, None),
            P(),
            P(),
            P("row", "col", None),
            P("row", "col", None),
            P("row", "col", None),
            P("row", "col", None),
            P("row", "col", None),
            P("row", "col", None),
            P("row", None),
            P("col", None),
            P("row", "col", None, None, None),
            P("row", "col", None, None, None),
            P("row", "col", None, None, None),
            P("row", "col", None, None, None),
        ),
        out_specs=(
            P("row", "col", None, None, None),
            P("row", "col", None, None, None),
            P("row", "col", None, None, None),
        ),
        check_vma=False,
    )
```

profile of v0, /device:TPU:8, one launch (start us, length us, event | category | flops | bytes accessed | tf_op | source)
XLA Modules:
  0.0 695.5 jit_solution(16541457742660147414)
XLA Ops:
  7.2 0.0 reduce-scatter.5.cloned.1.call-start
  7.2 0.7 compare_select_fusion.1
  7.9 0.7 compare_and_fusion.1
  8.5 1.0 copy.138
  9.6 0.7 iota_compare_fusion.1
  10.3 0.6 gather_fusion
  10.9 0.9 select_reduce_fusion.1
  11.7 0.0 copy-start.8
  11.7 0.0 copy-start.9
  11.8 0.0 copy-start.7
  11.8 2.9 fusion
  14.7 0.5 convolution_convert_fusion.3
  15.2 1.3 copy.67
  16.5 0.0 reduce-scatter.5.cloned.1.call-update
  16.5 0.0 reduce-scatter.7.cloned.1.call-start
  16.6 0.6 gather_fusion.1
  17.2 0.2 select_reduce_fusion
  17.4 0.1 iota_compare_fusion
  17.5 0.0 copy-start.2
  17.5 3.0 fusion.1
  20.5 0.5 convolution_convert_fusion.2
  21.0 1.3 copy.73
  22.3 0.0 reduce-scatter.7.cloned.1.call-update
  22.3 0.0 copy-start.5
  22.4 0.0 reduce-scatter.9.cloned.1.call-start
  22.4 0.1 copy.137
  22.5 133.0 %reduce-scatter.5.cloned.1.call-done = bf16[2,24,256]{2,1,0:T(8,128)(2,1)} async-done(((bf16[64,24,256]{2,1,0:T(8,128)(2,1)}), bf16[2,24,256]{2,1,0:T(8,128)(2,1)}) %reduce-scatter.5.cloned.1.call-update) | async-done | bytes 24592 | tf_op jit(solution)/shard_map/reduce_scatter | solution.py:119
  155.5 0.7 fusion.69
  156.3 0.0 copy-start.3
  156.3 0.0 copy-start.4
  156.3 22.9 %all_gather.12 = bf16[64,24,256]{2,1,0:T(8,128)(2,1)S(1)} all-gather(bf16[2,24,256]{2,1,0:T(8,128)(2,1)S(1)} %fusion.69), channel_id=1, replica_groups=mesh['row'=32,'col'=32] {'col'}, dimensions={0}, use_global_device_ids=true | all-gather | bytes 811008 | tf_op jit(solution)/shard_map/all_gather | solution.py:126
  179.2 0.3 fusion.25
  179.5 3.4 fusion.28
  182.9 0.6 fusion.23
  183.5 108.7 %reduce-scatter.7.cloned.1.call-done = bf16[2,24,256]{2,1,0:T(8,128)(2,1)} async-done(((bf16[64,24,256]{2,1,0:T(8,128)(2,1)}), bf16[2,24,256]{2,1,0:T(8,128)(2,1)}) %reduce-scatter.7.cloned.1.call-update) | async-done | bytes 24592 | tf_op jit(solution)/shard_map/reduce_scatter | solution.py:134
  292.2 0.7 fusion.66
  292.9 56.9 %all_gather.13 = bf16[64,24,256]{2,1,0:T(8,128)(2,1)S(1)} all-gather(bf16[2,24,256]{2,1,0:T(8,128)(2,1)S(1)} %fusion.66), channel_id=1, replica_groups=mesh['row'=32,'col'=32] {'row'}, dimensions={0}, use_global_device_ids=true | all-gather | bytes 811008 | tf_op jit(solution)/shard_map/all_gather | solution.py:141
  349.9 0.3 fusion.21
  350.2 3.4 fusion.31
  353.6 0.6 fusion.114
  354.3 0.6 gather_fusion.2
  354.8 2.9 fusion.2
  357.8 0.5 convolution_convert_fusion.1
  358.2 1.3 copy.79
  359.6 0.0 reduce-scatter.9.cloned.1.call-update
  359.6 0.0 reduce-scatter.11.cloned.1.call-start
  359.6 0.6 gather_fusion.3
  360.2 2.9 fusion.3
  363.1 0.5 convolution_convert_fusion
  363.6 1.3 copy.85
  365.0 0.0 reduce-scatter.11.cloned.1.call-update
  365.0 123.3 %reduce-scatter.9.cloned.1.call-done = bf16[2,24,256]{2,1,0:T(8,128)(2,1)} async-done(((bf16[64,24,256]{2,1,0:T(8,128)(2,1)}), bf16[2,24,256]{2,1,0:T(8,128)(2,1)}) %reduce-scatter.9.cloned.1.call-update) | async-done | bytes 24592 | tf_op jit(solution)/shard_map/reduce_scatter | solution.py:119
  488.3 1.4 fusion.91
  489.7 23.1 %all_gather.14 = bf16[64,24,256]{2,1,0:T(8,128)(2,1)S(1)} all-gather(bf16[2,24,256]{2,1,0:T(8,128)(2,1)S(1)} %get-tuple-element.19), channel_id=1, replica_groups=mesh['row'=32,'col'=32] {'col'}, dimensions={0}, use_global_device_ids=true | all-gather | bytes 811008 | tf_op jit(solution)/shard_map/all_gather | solution.py:126
  512.8 0.3 fusion.18
  513.1 3.4 fusion.34
  516.5 0.6 fusion.16
  517.1 108.5 %reduce-scatter.11.cloned.1.call-done = bf16[2,24,256]{2,1,0:T(8,128)(2,1)} async-done(((bf16[64,24,256]{2,1,0:T(8,128)(2,1)}), bf16[2,24,256]{2,1,0:T(8,128)(2,1)}) %reduce-scatter.11.cloned.1.call-update) | async-done | bytes 24592 | tf_op jit(solution)/shard_map/reduce_scatter | solution.py:134
  625.6 1.4 fusion.93
  627.0 57.0 %all_gather.15 = bf16[64,24,256]{2,1,0:T(8,128)(2,1)S(1)} all-gather(bf16[2,24,256]{2,1,0:T(8,128)(2,1)S(1)} %get-tuple-element.17), channel_id=1, replica_groups=mesh['row'=32,'col'=32] {'row'}, dimensions={0}, use_global_device_ids=true | all-gather | bytes 811008 | tf_op jit(solution)/shard_map/all_gather | solution.py:141
  683.9 0.3 fusion.14
  684.3 3.4 fusion.37
  687.7 0.6 fusion.12
  688.3 0.7 copy.89
  (21 shorter events, 0.1 us)
Async XLA Ops:
  7.2 148.3 %reduce-scatter.5.cloned.1.call-start = ((), (), s32[]{:S(2)}) async-start(), calls=%async_computation.4 | async-start | bytes 811008 | tf_op jit(solution)/shard_map/reduce_scatter | solution.py:119
  11.7 4.9 copy-start.6
  11.7 5.5 copy-start.8
  11.7 5.5 copy-start.9
  11.8 5.7 copy-start.7
  16.5 275.6 %reduce-scatter.7.cloned.1.call-start = ((), (), s32[]{:S(2)}) async-start(), calls=%async_computation.5 | async-start | bytes 811008 | tf_op jit(solution)/shard_map/reduce_scatter | solution.py:134
  17.5 4.9 copy-start
  17.5 138.0 %copy-start.1 = (f32[1,1,2,24,256]{4,3,2,1,0:T(8,128)S(1)}, f32[1,1,2,24,256]{4,3,2,1,0:T(8,128)}, u32[]{:S(2)}) copy-start(f32[1,1,2,24,256]{4,3,2,1,0:T(8,128)} %param.28) | copy-start | bytes 147460
  17.5 138.0 %copy-start.2 = (f32[1,1,2,24,256]{4,3,2,1,0:T(8,128)S(1)}, f32[1,1,2,24,256]{4,3,2,1,0:T(8,128)}, u32[]{:S(2)}) copy-start(f32[1,1,2,24,256]{4,3,2,1,0:T(8,128)} %param.30) | copy-start | bytes 147460
  22.3 160.6 %copy-start.5 = (s32[1,1,32]{2,1,0:T(1,128)S(1)}, s32[1,1,32]{2,1,0:T(1,128)}, u32[]{:S(2)}) copy-start(s32[1,1,32]{2,1,0:T(1,128)} %param.20) | copy-start | bytes 388
  22.4 466.0 %reduce-scatter.9.cloned.1.call-start = ((), (), s32[]{:S(2)}) async-start(), calls=%async_computation.6 | async-start | bytes 811008 | tf_op jit(solution)/shard_map/reduce_scatter | solution.py:119
  156.3 135.9 %copy-start.3 = (f32[1,1,2,24,256]{4,3,2,1,0:T(8,128)S(1)}, f32[1,1,2,24,256]{4,3,2,1,0:T(8,128)}, u32[]{:S(2)}) copy-start(f32[1,1,2,24,256]{4,3,2,1,0:T(8,128)} %param.29) | copy-start | bytes 147460
  156.3 135.9 %copy-start.4 = (f32[1,1,2,24,256]{4,3,2,1,0:T(8,128)S(1)}, f32[1,1,2,24,256]{4,3,2,1,0:T(8,128)}, u32[]{:S(2)}) copy-start(f32[1,1,2,24,256]{4,3,2,1,0:T(8,128)} %param.31) | copy-start | bytes 147460
  359.6 266.0 %reduce-scatter.11.cloned.1.call-start = ((), (), s32[]{:S(2)}) async-start(), calls=%async_computation.7 | async-start | bytes 811008 | tf_op jit(solution)/shard_map/reduce_scatter | solution.py:134
Sparse Core Ops, SparseCore 0:
  16.7 138.7 reduce-scatter.4
  158.9 133.2 reduce-scatter.6
  359.7 128.5 reduce-scatter.8
  491.9 133.6 reduce-scatter.10
where the time goes:
time: 696 us
  waiting for transfers between devices  474 us (68%)
  blocking collectives  160 us (23%)
  matrix products  30.9 us (4%)
  between operations  14.1 us (2%)
  local copies, waits for them, and re-layouts  9.5 us (1%)
  other arithmetic  7.44 us (1%)
    reduce_scatter x2, waiting for transfers between devices, shards(): lax.psum_scatter(term_fn(jnp.int32(0), num_rows * lax.axis_size('col')).a...  256 us
    reduce_scatter x2, waiting for transfers between devices, shards(): lax.psum_scatter(term_fn(jnp.int32(0), num_rows * lax.axis_size('row')).a...  217 us
    all_gather x2, blocking collectives, shards(): lax.all_gather(values, 'row', axis=0, tiled=True)  114 us
    all_gather x2, blocking collectives, shards(): lax.all_gather(values, 'col', axis=0, tiled=True)  46 us
  transfers between devices with their start and end apart: 4, of which 4 were waited for; matrix products, arithmetic and copies ran while one was open for 3% of the time, Pallas kernels for 0%

commit v1 on v0

v1 whole, which is shorter than its diff:
```python
import functools

import jax
import jax.numpy as jnp
from jax import lax
from jax.experimental import pallas as pl
from jax.experimental.pallas import tpu as pltpu
from jax.sharding import PartitionSpec as P

OWNED = 2
ITERS = 2
RING = 4

HUBER_DELTA = 0.5
STEP_SIZE = 0.05
SMOOTH_WEIGHT = 1.0

F32 = jnp.float32
BF16 = jnp.bfloat16

SLOT, TILE_OF, FOOT, OWNER, ODD, SAME, INVERSE, LAST = range(8)


def slot_tables(ray_list, owner_row, tiles, footprint, num_tiles):
    positions = owner_row.shape[0]
    slots = ray_list.shape[0]
    ids = jnp.arange(slots, dtype=jnp.int32)
    earlier = ids[None, :] < ids[:, None]
    before = (tiles[None, :] < tiles[:, None]) | ((tiles[None, :] == tiles[:, None]) & earlier)
    rank = jnp.sum(before.astype(jnp.int32), axis=1)
    named = ray_list[:, None] == jnp.arange(positions, dtype=jnp.int32)[None, :]
    position = jnp.sum(jnp.where(named, owner_row[None, :], 0), axis=1)
    here = rank[None, :] == ids[:, None]

    def sort(values):
        return jnp.sum(jnp.where(here, values[None, :], 0), axis=1)

    slot = sort(ids)
    tile = sort(tiles)
    foot = sort(footprint)
    pos = sort(position)
    same = jnp.concatenate([jnp.zeros((1,), jnp.int32), (tile[1:] == tile[:-1]).astype(jnp.int32)])
    holds = pos[None, :] == jnp.arange(positions, dtype=jnp.int32)[:, None]
    inverse = slots - jnp.sum(jnp.where(holds, slots - ids[None, :], 0), axis=1)
    tile_ids = jnp.arange(num_tiles, dtype=jnp.int32)
    upto = jnp.sum((tiles[None, :] <= tile_ids[:, None]).astype(jnp.int32), axis=1)
    present = jnp.any(tiles[None, :] == tile_ids[:, None], axis=1)
    last = jnp.where(present, upto - 1, slots)
    width = max(positions, slots, num_tiles)

    def row(values):
        return jnp.pad(values.astype(jnp.int32), (0, width - values.shape[0]))

    return jnp.stack(
        [row(v) for v in (slot, tile, foot, pos // OWNED, pos % OWNED, same, inverse, last)]
    )


def body(
    n_row,
    n_col,
    tab_a,
    tab_d,
    vol,
    blk_a_hbm,
    blk_d_hbm,
    meas_a,
    meas_d,
    wt_a,
    wt_d,
    vol_out,
    res_a,
    res_d,
    blk_a,
    blk_d,
    part_a,
    part_d,
    cum_a,
    cum_d,
    smooth,
    gat_a,
    gat_d,
    send_a,
    recv_a,
    sp,
    rp,
    sm,
    rm,
    hub,
    half_s,
    half_r,
    full_s,
    full_r,
    blk_sem,
    ca_s,
    ca_r,
    cg_s,
    cg_r,
    sp_s,
    sp_r,
    sm_s,
    sm_r,
    h_s,
    h_r,
    f_s,
    f_r,
    gf_s,
    gf_r,
    gh_s,
    gh_r,
    gp_s,
    gp_r,
    gm_s,
    gm_r,
):
    z = lax.axis_index("row")
    c = lax.axis_index("col")
    num_tiles, slices, _ = vol.shape
    slots_a = blk_a.shape[0]
    slots_d = blk_d.shape[0]
    rays = blk_a.shape[2]
    lanes = rays // 2
    gap = n_row // RING
    up_steps = gap // 2
    down_steps = gap // 2 - 1

    def zrow(offset):
        return lax.rem(z + (offset % n_row), n_row)

    def zdev(offset):
        return (zrow(offset), c)

    def ccol(k):
        return lax.rem(c + k, n_col)

    def remote(src, dst, s_sem, r_sem, dev):
        return pltpu.make_async_remote_copy(
            src_ref=src,
            dst_ref=dst,
            send_sem=s_sem,
            recv_sem=r_sem,
            device_id=dev,
            device_id_type=pl.DeviceIdType.MESH,
        )

    loads = (
        pltpu.make_async_copy(blk_d_hbm, blk_d, blk_sem.at[0]),
        pltpu.make_async_copy(blk_a_hbm, blk_a, blk_sem.at[1]),
    )
    for load in loads:
        load.start()

    barrier = pltpu.get_barrier_semaphore()

    def greet(k, carry):
        pl.semaphore_signal(
            barrier, inc=1, device_id=(z, ccol(k)), device_id_type=pl.DeviceIdType.MESH
        )
        return carry

    for offset in (gap, -gap, 1, -1):
        pl.semaphore_signal(
            barrier, inc=1, device_id=zdev(offset), device_id_type=pl.DeviceIdType.MESH
        )
    lax.fori_loop(1, n_col, greet, 0)

    zero = jnp.zeros((slices, rays), F32)
    part_a[slots_a] = zero
    part_d[slots_d] = zero
    cum_a[slots_a] = zero
    cum_d[slots_d] = zero
    for k in range(num_tiles):
        vol_out[k] = vol[k]

    ray_index = lax.broadcasted_iota(jnp.int32, (slices, rays), 1)
    slice_index = lax.broadcasted_iota(jnp.int32, (slices, rays), 0)

    def forward(tab, blk, part, first, count):
        def one(j, carry):
            tile = vol_out[tab[TILE_OF, j]].astype(BF16)
            value = jnp.dot(tile, blk[tab[SLOT, j]], preferred_element_type=F32)
            part[j] = jnp.where(ray_index < tab[FOOT, j], value, 0.0)
            return carry

        lax.fori_loop(first, first + count, one, 0, unroll=min(4, count))

    def backward(tab, blk, gat, cum, first, count):
        def one(j, total):
            both = gat[tab[OWNER, j]].astype(F32)
            items = jnp.where(tab[ODD, j] == 1, both[slices:], both[:slices])
            items = jnp.where(ray_index < tab[FOOT, j], items, 0.0).astype(BF16)
            value = lax.dot_general(
                items, blk[tab[SLOT, j]], (((1,), (1,)), ((), ())), preferred_element_type=F32
            )
            total = jnp.where(tab[SAME, j] == 1, total, 0.0) + value
            cum[j] = total
            return total

        start = cum[first - 1] if first else zero
        lax.fori_loop(first, first + count, one, start, unroll=min(4, count))

    def own(tab, part, owner):
        return jnp.concatenate(
            [part[tab[INVERSE, 2 * owner]], part[tab[INVERSE, 2 * owner + 1]]], axis=0
        )

    def own_d(owner):
        return own(tab_d, part_d, owner)

    def own_a(owner):
        return own(tab_a, part_a, owner)

    def smoothing():
        for k in range(num_tiles):
            x = vol_out[k]
            step = pltpu.roll(x, slices - 1, 0) - x
            slope = jnp.clip(step, -HUBER_DELTA, HUBER_DELTA)
            slope = jnp.where(slice_index < slices - 1, slope, 0.0)
            smooth[k] = pltpu.roll(slope, 1, 0) - slope

    parts = 4
    per = slots_a // parts if slots_a % parts == 0 else slots_a

    def pieces(fn):
        return [functools.partial(fn, i * per, per) for i in range(slots_a // per)]

    def send_across():
        def one(k, carry):
            send_a[k] = own_a(ccol(k)).astype(BF16)
            remote(send_a.at[k], recv_a.at[k], ca_s.at[k], ca_r.at[k], (z, ccol(k))).start()
            return carry

        lax.fori_loop(1, n_col, one, 0)

    def finish_across():
        def one(k, total):
            remote(send_a.at[k], recv_a.at[k], ca_s.at[k], ca_r.at[k], (z, ccol(k))).wait_recv()
            return total + recv_a[k].astype(F32)

        projection = lax.fori_loop(1, n_col, one, own_a(c))
        residual = wt_a[...] * (meas_a[...] - projection)
        res_a[...] = residual
        gat_a[c] = residual.astype(BF16)

        def spread(k, carry):
            remote(gat_a.at[c], gat_a.at[c], cg_s.at[k], cg_r.at[k], (z, ccol(k))).start()
            return carry

        lax.fori_loop(1, n_col, spread, 0)

    def collect_across():
        def one(k, carry):
            remote(gat_a.at[c], gat_a.at[c], cg_s.at[k], cg_r.at[k], (z, ccol(k))).wait_recv()
            return carry

        lax.fori_loop(1, n_col, one, 0)

    def drain_across():
        def one(k, carry):
            remote(send_a.at[k], recv_a.at[k], ca_s.at[k], ca_r.at[k], (z, ccol(k))).wait_send()
            remote(gat_a.at[c], gat_a.at[c], cg_s.at[k], cg_r.at[k], (z, ccol(k))).wait_send()
            return carry

        lax.fori_loop(1, n_col, one, 0)

    def plus(t, k):
        return remote(sp.at[t, k], rp.at[t, k], sp_s.at[t, k], sp_r.at[t, k], zdev(1))

    def minus(t, k):
        return remote(sm.at[t, k], rm.at[t, k], sm_s.at[t, k], sm_r.at[t, k], zdev(-1))

    def half(i):
        return remote(half_s.at[i], half_r.at[i], h_s.at[i], h_r.at[i], zdev(gap if i == 0 else -gap))

    def full(i):
        return remote(full_s.at[i], full_r.at[i], f_s.at[i], f_r.at[i], zdev(gap if i == 0 else -gap))

    def chain_step(t, k):
        value = own_d(zrow(up_steps - t + gap * k))
        if t:
            plus(t - 1, k).wait_recv()
            value = value + rp[t - 1, k].astype(F32)
        sp[t, k] = value.astype(BF16)
        plus(t, k).start()
        if t < down_steps:
            value = own_d(zrow(t - down_steps + gap * k))
            if t:
                minus(t - 1, k).wait_recv()
                value = value + rm[t - 1, k].astype(F32)
            sm[t, k] = value.astype(BF16)
            minus(t, k).start()

    def hub_total(k):
        value = own_d(zrow(gap * k))
        if down_steps:
            minus(down_steps - 1, k).wait_recv()
            value = value + rm[down_steps - 1, k].astype(F32)
        plus(up_steps - 1, k).wait_recv()
        return value + rp[up_steps - 1, k].astype(F32)

    def reduce_down(fillers):
        fillers = list(fillers)
        for t in range(up_steps):
            for k in (2, 1, 3):
                chain_step(t, k)
            if fillers:
                fillers.pop(0)()
        value = hub_total(2)
        half_s[0] = value[:, :lanes].astype(BF16)
        half_s[1] = value[:, lanes:].astype(BF16)
        half(0).start()
        half(1).start()
        for filler in fillers:
            filler()
        send_across()
        hub[0] = hub_total(1)
        hub[1] = hub_total(3)
        for t in range(up_steps):
            chain_step(t, 0)
        smoothing()
        hub[2] = hub_total(0)
        half(0).wait_recv()
        value = hub[0]
        full_s[0, :, :lanes] = (value[:, :lanes] + half_r[0].astype(F32)).astype(BF16)
        full_s[0, :, lanes:] = value[:, lanes:].astype(BF16)
        full(0).start()
        half(1).wait_recv()
        value = hub[1]
        full_s[1, :, :lanes] = value[:, :lanes].astype(BF16)
        full_s[1, :, lanes:] = (value[:, lanes:] + half_r[1].astype(F32)).astype(BF16)
        full(1).start()
        finish_across()
        full(0).wait_recv()
        full(1).wait_recv()
        projection = hub[2] + full_r[0].astype(F32) + full_r[1].astype(F32)
        residual = wt_d[...] * (meas_d[...] - projection)
        res_d[...] = residual
        gat_d[z] = residual.astype(BF16)

    def out_full(i, offset):
        mine = gat_d.at[zrow(offset)]
        return remote(mine, mine, gf_s.at[i], gf_r.at[i], zdev(gap if i == 0 else -gap))

    def out_half(i):
        owner = zrow(-gap if i == 0 else gap)
        piece = gat_d.at[owner, :, pl.ds(i * lanes, lanes)]
        return remote(piece, piece, gh_s.at[i], gh_r.at[i], zdev(gap if i == 0 else -gap))

    def out_minus(t, k):
        shard = gat_d.at[zrow(t + gap * k)]
        return remote(shard, shard, gm_s.at[t, k], gm_r.at[t, k], zdev(-1))

    def out_plus(t, k):
        shard = gat_d.at[zrow(gap * k - t)]
        return remote(shard, shard, gp_s.at[t, k], gp_r.at[t, k], zdev(1))

    def out_step(t, k):
        if t:
            out_minus(t - 1, k).wait_recv()
        out_minus(t, k).start()
        if t < down_steps:
            if t:
                out_plus(t - 1, k).wait_recv()
            out_plus(t, k).start()

    def out_last(k):
        out_minus(up_steps - 1, k).wait_recv()
        if down_steps:
            out_plus(down_steps - 1, k).wait_recv()

    def spread_down(fillers):
        fillers = list(fillers)
        out_full(0, 0).start()
        out_full(1, 0).start()
        for t in range(up_steps):
            out_step(t, 0)
        out_full(0, 0).wait_recv()
        out_half(0).start()
        out_full(1, 0).wait_recv()
        out_half(1).start()
        for k in (1, 3):
            out_step(0, k)
        collect_across()
        for t in range(1, up_steps):
            if fillers:
                fillers.pop(0)()
            for k in (1, 3):
                out_step(t, k)
        for filler in fillers:
            filler()
        out_half(0).wait_recv()
        out_half(1).wait_recv()
        for t in range(up_steps):
            out_step(t, 2)
        for k in (0, 1, 3, 2):
            out_last(k)

    def drain_down():
        for k in range(RING):
            for t in range(up_steps):
                plus(t, k).wait_send()
                out_minus(t, k).wait_send()
            for t in range(down_steps):
                minus(t, k).wait_send()
                out_plus(t, k).wait_send()
        for i in range(2):
            half(i).wait_send()
            full(i).wait_send()
            out_full(i, 0).wait_send()
            out_half(i).wait_send()

    loads[0].wait()
    forward(tab_d, blk_d, part_d, 0, slots_d)
    loads[1].wait()
    pl.semaphore_wait(barrier, n_col - 1 + 4)

    def iteration(step, carry):
        reduce_down(pieces(functools.partial(forward, tab_a, blk_a, part_a)))
        spread_down(pieces(functools.partial(backward, tab_a, blk_a, gat_a, cum_a)))
        backward(tab_d, blk_d, gat_d, cum_d, 0, slots_d)
        for k in range(num_tiles):
            gradient = cum_a[tab_a[LAST, k]] + cum_d[tab_d[LAST, k]]
            x = vol_out[k]
            vol_out[k] = jnp.maximum(
                x + STEP_SIZE * (gradient - SMOOTH_WEIGHT * smooth[k]), 0.0
            )
        drain_across()
        drain_down()

        @pl.when(step < ITERS - 1)
        def _():
            forward(tab_d, blk_d, part_d, 0, slots_d)

        return carry

    lax.fori_loop(0, ITERS, iteration, 0)


def shards(
    n_row,
    n_col,
    volume,
    blocks_across,
    downward_ray_blocks,
    tiles_across,
    tiles_down,
    footprint_across,
    footprint_down,
    rays_across,
    rays_down,
    owners_across,
    owners_down,
    observed_sinogram_across,
    observed_sinogram_down,
    weights_across,
    weights_down,
):
    voxels = volume[0, 0]
    num_tiles, slices, tile = voxels.shape
    slots_a, _, rays = blocks_across.shape
    slots_d = downward_ray_blocks.shape[0]
    rows = OWNED * slices
    tab_a = slot_tables(
        rays_across[0, 0], owners_across[0], tiles_across[0, 0], footprint_across[0, 0], num_tiles
    )
    tab_d = slot_tables(
        rays_down[0, 0], owners_down[0], tiles_down[0, 0], footprint_down[0, 0], num_tiles
    )
    gap = n_row // RING
    up_steps = gap // 2
    down_steps = max(gap // 2 - 1, 1)
    dma = pltpu.SemaphoreType.DMA

    def shard(*lead):
        return pltpu.VMEM((*lead, rows, rays), BF16)

    vmem = pl.BlockSpec(memory_space=pltpu.VMEM)
    smem = pl.BlockSpec(memory_space=pltpu.SMEM)
    anywhere = pl.BlockSpec(memory_space=pl.ANY)
    own_shape = jax.ShapeDtypeStruct((rows, rays), F32)
    outs = pl.pallas_call(
        functools.partial(body, n_row, n_col),
        out_shape=(jax.ShapeDtypeStruct(voxels.shape, F32), own_shape, own_shape),
        in_specs=[smem, smem, vmem, anywhere, anywhere, vmem, vmem, vmem, vmem],
        out_specs=(vmem, vmem, vmem),
        scratch_shapes=[
            pltpu.VMEM(blocks_across.shape, BF16),
            pltpu.VMEM(downward_ray_blocks.shape, BF16),
            pltpu.VMEM((slots_a + 1, slices, rays), F32),
            pltpu.VMEM((slots_d + 1, slices, rays), F32),
            pltpu.VMEM((slots_a + 1, slices, tile), F32),
            pltpu.VMEM((slots_d + 1, slices, tile), F32),
            pltpu.VMEM(voxels.shape, F32),
            shard(n_col),
            shard(n_row),
            shard(n_col),
            shard(n_col),
            shard(up_steps, RING),
            shard(up_steps, RING),
            shard(down_steps, RING),
            shard(down_steps, RING),
            pltpu.VMEM((3, rows, rays), F32),
            pltpu.VMEM((2, rows, rays // 2), BF16),
            pltpu.VMEM((2, rows, rays // 2), BF16),
            shard(2),
            shard(2),
            dma((2,)),
            dma((n_col,)),
            dma((n_col,)),
            dma((n_col,)),
            dma((n_col,)),
            dma((up_steps, RING)),
            dma((up_steps, RING)),
            dma((down_steps, RING)),
            dma((down_steps, RING)),
            dma((2,)),
            dma((2,)),
            dma((2,)),
            dma((2,)),
            dma((2,)),
            dma((2,)),
            dma((2,)),
            dma((2,)),
            dma((down_steps, RING)),
            dma((down_steps, RING)),
            dma((up_steps, RING)),
            dma((up_steps, RING)),
        ],
        compiler_params=pltpu.CompilerParams(
            collective_id=0, has_side_effects=True, vmem_limit_bytes=48 << 20
        ),
        name="tomography",
    )(
        tab_a,
        tab_d,
        voxels,
        blocks_across,
        downward_ray_blocks,
        observed_sinogram_across.reshape(rows, rays),
        observed_sinogram_down.reshape(rows, rays),
        weights_across.reshape(rows, rays),
        weights_down.reshape(rows, rays),
    )
    shape = observed_sinogram_across.shape
    return (outs[0][None, None], outs[1].reshape(shape), outs[2].reshape(shape))


def solution(mesh):
    return jax.shard_map(
        functools.partial(shards, mesh.shape["row"], mesh.shape["col"]),
        mesh=mesh,
        in_specs=(
            P("row", "col", None, None, None),
            P(),
            P(),
            P("row", "col", None),
            P("row", "col", None),
            P("row", "col", None),
            P("row", "col", None),
            P("row", "col", None),
            P("row", "col", None),
            P("row", None),
            P("col", None),
            P("row", "col", None, None, None),
            P("row", "col", None, None, None),
            P("row", "col", None, None, None),
            P("row", "col", None, None, None),
        ),
        out_specs=(
            P("row", "col", None, None, None),
            P("row", "col", None, None, None),
            P("row", "col", None, None, None),
        ),
        check_vma=False,
    )
```

time: 696 us -> 189 us (0.27)
  the two profiles are of different devices: /device:TPU:8 before, /device:TPU:42 now
where the time goes in v1:
time: 189 us
  Pallas kernels  171 us (90%)
  other arithmetic  8.66 us (5%)
  local copies, waits for them, and re-layouts  8.3 us (4%)
    pallas_call x1, Pallas kernels, shards(): pl.pallas_call(functools.partial(body, n_row, n_col), out_shape=(jax.Shap...  171 us
    unnamed x15, local copies, waits for them, and re-layouts  8.22 us

profile of v1, /device:TPU:42, one launch (start us, length us, event | category | flops | bytes accessed | tf_op | source)
XLA Modules:
  0.0 188.7 jit_solution(12032571415445522389)
XLA Ops:
  0.6 0.8 convert_reduce_fusion.3
  1.4 0.8 fusion.4
  2.2 0.9 convert_reduce_fusion.1
  3.1 0.8 convert_reduce_fusion.2
  3.9 0.8 fusion.5
  4.7 0.9 convert_reduce_fusion
  5.6 0.9 select_reduce_fusion.8
  6.4 0.9 select_reduce_fusion.2
  7.3 0.8 select_reduce_fusion.1
  8.1 0.1 slice_compare_fusion
  8.2 0.8 select_reduce_fusion.7
  9.0 0.1 slice_compare_fusion.1
  9.1 0.1 pad_add_fusion
  9.2 0.1 select_reduce_fusion
  9.4 0.0 copy-start
  9.5 2.2 %copy-done = bf16[32,256,256]{2,1,0:T(8,128)(2,1)S(1)} copy-done((bf16[32,256,256]{2,1,0:T(8,128)(2,1)S(1)}, bf16[32,256,256]{2,1,0:T(8,128)(2,1)}, u32[]{:S(2)}) %copy-start) | copy-done | bytes 4194328
  11.6 0.0 copy-start.1
  11.6 0.9 copy-done.1
  12.6 0.0 copy-start.2
  12.6 0.8 copy-done.2
  13.4 0.0 copy-start.3
  13.4 0.8 copy-done.3
  14.2 0.0 copy-start.4
  14.2 0.8 copy-done.4
  15.0 0.0 copy-start.5
  15.0 0.8 copy-done.5
  15.8 171.0 %tomography.1 = (f32[8,24,256]{2,1,0:T(8,128)S(1)}, f32[48,256]{1,0:T(8,128)S(1)}, f32[48,256]{1,0:T(8,128)S(1)}) custom-call(s32[8,64]{1,0:T(8,128)S(1)} %stack.64.tab_a, s32[8,64]{1,0:T(8,128)S(1)} %stack.73.tab_d, f32[8,24,256]{2,1,0:T(8,128)S(1)} %bitcast.49, bf16[32,256,256]{2,1,0:T(8,128)(2,1)S(1)} %copy-done, bf16[32,256,256]{2,1,0:T(8,128)(2,1)} %blk_d_hbm.1, ...), custom_call_target="tpu_custom_call" | custom-call | tf_op jit(solution)/shard_map/tomography/pallas_call | solution.py:481
  186.7 0.7 copy.21
  187.4 0.6 copy.22
  188.0 0.6 copy.23
  (16 shorter events, 0.1 us)
Async XLA Ops:
  9.4 2.2 %copy-start = (bf16[32,256,256]{2,1,0:T(8,128)(2,1)S(1)}, bf16[32,256,256]{2,1,0:T(8,128)(2,1)}, u32[]{:S(2)}) copy-start(bf16[32,256,256]{2,1,0:T(8,128)(2,1)} %blk_a_hbm.1) | copy-start | bytes 12582916
  11.6 0.9 copy-start.1
  12.6 0.8 copy-start.2
  13.4 0.8 copy-start.3
  14.2 0.8 copy-start.4
  15.0 0.8 copy-start.5

commit v2 on v1

--- a/solution.py
+++ b/solution.py
@@ -21,7 +21,7 @@
 SLOT, TILE_OF, FOOT, OWNER, ODD, SAME, INVERSE, LAST = range(8)
 
 
-def slot_tables(ray_list, owner_row, tiles, footprint, num_tiles):
+def slot_tables(num_tiles, ray_list, owner_row, tiles, footprint):
     positions = owner_row.shape[0]
     slots = ray_list.shape[0]
     ids = jnp.arange(slots, dtype=jnp.int32)
@@ -64,15 +64,19 @@
     vol,
     blk_a_hbm,
     blk_d_hbm,
-    meas_a,
-    meas_d,
-    wt_a,
-    wt_d,
+    meas_a_hbm,
+    meas_d_hbm,
+    wt_a_hbm,
+    wt_d_hbm,
     vol_out,
     res_a,
     res_d,
     blk_a,
     blk_d,
+    meas_a,
+    meas_d,
+    wt_a,
+    wt_d,
     part_a,
     part_d,
     cum_a,
@@ -80,6 +84,8 @@
     smooth,
     gat_a,
     gat_d,
+    twin_s,
+    twin_r,
     send_a,
     recv_a,
     sp,
@@ -92,6 +98,10 @@
     full_s,
     full_r,
     blk_sem,
+    tw_s,
+    tw_r,
+    tg_s,
+    tg_r,
     ca_s,
     ca_r,
     cg_s,
@@ -130,8 +140,16 @@
     def zdev(offset):
         return (zrow(offset), c)
 
-    def ccol(k):
-        return lax.rem(c + k, n_col)
+    chips = n_col // 2
+    core = lax.rem(c, 2)
+    chip = (c - core) // 2
+    twin = (z, c + 1 - 2 * core)
+
+    def ccol(k, side):
+        return 2 * lax.rem(chip + k, chips) + side
+
+    def cdev(k):
+        return (z, ccol(k, core))
 
     def remote(src, dst, s_sem, r_sem, dev):
         return pltpu.make_async_remote_copy(
@@ -143,10 +161,16 @@
             device_id_type=pl.DeviceIdType.MESH,
         )
 
-    loads = (
-        pltpu.make_async_copy(blk_d_hbm, blk_d, blk_sem.at[0]),
-        pltpu.make_async_copy(blk_a_hbm, blk_a, blk_sem.at[1]),
+    pairs = (
+        (vol, vol_out),
+        (blk_d_hbm, blk_d),
+        (blk_a_hbm, blk_a),
+        (meas_d_hbm, meas_d),
+        (wt_d_hbm, wt_d),
+        (meas_a_hbm, meas_a),
+        (wt_a_hbm, wt_a),
     )
+    loads = [pltpu.make_async_copy(src, dst, blk_sem.at[i]) for i, (src, dst) in enumerate(pairs)]
     for load in loads:
         load.start()
 
@@ -154,7 +178,7 @@
 
     def greet(k, carry):
         pl.semaphore_signal(
-            barrier, inc=1, device_id=(z, ccol(k)), device_id_type=pl.DeviceIdType.MESH
+            barrier, inc=1, device_id=cdev(k), device_id_type=pl.DeviceIdType.MESH
         )
         return carry
 
@@ -162,15 +186,14 @@
         pl.semaphore_signal(
             barrier, inc=1, device_id=zdev(offset), device_id_type=pl.DeviceIdType.MESH
         )
-    lax.fori_loop(1, n_col, greet, 0)
+    pl.semaphore_signal(barrier, inc=1, device_id=twin, device_id_type=pl.DeviceIdType.MESH)
+    lax.fori_loop(1, chips, greet, 0)
 
     zero = jnp.zeros((slices, rays), F32)
     part_a[slots_a] = zero
     part_d[slots_d] = zero
     cum_a[slots_a] = zero
     cum_d[slots_d] = zero
-    for k in range(num_tiles):
-        vol_out[k] = vol[k]
 
     ray_index = lax.broadcasted_iota(jnp.int32, (slices, rays), 1)
     slice_index = lax.broadcasted_iota(jnp.int32, (slices, rays), 0)
@@ -224,44 +247,72 @@
     def pieces(fn):
         return [functools.partial(fn, i * per, per) for i in range(slots_a // per)]
 
+    def twin_part():
+        return remote(twin_s, twin_r, tw_s.at[0], tw_r.at[0], twin)
+
+    def across_part(k):
+        return remote(send_a.at[k], recv_a.at[k], ca_s.at[k], ca_r.at[k], cdev(k))
+
+    def across_out(k):
+        return remote(gat_a.at[c], gat_a.at[c], cg_s.at[k], cg_r.at[k], cdev(k))
+
+    def twin_out(k):
+        shard = gat_a.at[ccol(chips - k, core)]
+        return remote(shard, shard, tg_s.at[k], tg_r.at[k], twin)
+
+    def each_chip(first, fn):
+        def one(k, carry):
+            fn(k)
+            return carry
+
+        lax.fori_loop(first, chips, one, 0)
+
+    def start_across():
+        def stage(k):
+            twin_s[k] = own_a(ccol(k, 1 - core)).astype(BF16)
+
+        each_chip(0, stage)
+        twin_part().start()
+
     def send_across():
-        def one(k, carry):
-            send_a[k] = own_a(ccol(k)).astype(BF16)
-            remote(send_a.at[k], recv_a.at[k], ca_s.at[k], ca_r.at[k], (z, ccol(k))).start()
-            return carry
-
-        lax.fori_loop(1, n_col, one, 0)
+        twin_part().wait_recv()
+
+        def stage(k):
+            send_a[k] = (own_a(ccol(k, core)) + twin_r[k].astype(F32)).astype(BF16)
+            across_part(k).start()
+
+        each_chip(1, stage)
 
     def finish_across():
         def one(k, total):
-            remote(send_a.at[k], recv_a.at[k], ca_s.at[k], ca_r.at[k], (z, ccol(k))).wait_recv()
+            across_part(k).wait_recv()
             return total + recv_a[k].astype(F32)
 
-        projection = lax.fori_loop(1, n_col, one, own_a(c))
+        projection = lax.fori_loop(1, chips, one, own_a(c) + twin_r[0].astype(F32))
         residual = wt_a[...] * (meas_a[...] - projection)
         res_a[...] = residual
         gat_a[c] = residual.astype(BF16)
-
-        def spread(k, carry):
-            remote(gat_a.at[c], gat_a.at[c], cg_s.at[k], cg_r.at[k], (z, ccol(k))).start()
-            return carry
-
-        lax.fori_loop(1, n_col, spread, 0)
+        each_chip(1, lambda k: across_out(k).start())
+        twin_out(0).start()
+
+    def pass_across():
+        def relay(k):
+            across_out(k).wait_recv()
+            twin_out(k).start()
+
+        each_chip(1, relay)
 
     def collect_across():
-        def one(k, carry):
-            remote(gat_a.at[c], gat_a.at[c], cg_s.at[k], cg_r.at[k], (z, ccol(k))).wait_recv()
-            return carry
-
-        lax.fori_loop(1, n_col, one, 0)
+        each_chip(0, lambda k: twin_out(k).wait_recv())
 
     def drain_across():
-        def one(k, carry):
-            remote(send_a.at[k], recv_a.at[k], ca_s.at[k], ca_r.at[k], (z, ccol(k))).wait_send()
-            remote(gat_a.at[c], gat_a.at[c], cg_s.at[k], cg_r.at[k], (z, ccol(k))).wait_send()
-            return carry
-
-        lax.fori_loop(1, n_col, one, 0)
+        def one(k):
+            across_part(k).wait_send()
+            across_out(k).wait_send()
+
+        each_chip(1, one)
+        each_chip(0, lambda k: twin_out(k).wait_send())
+        twin_part().wait_send()
 
     def plus(t, k):
         return remote(sp.at[t, k], rp.at[t, k], sp_s.at[t, k], sp_r.at[t, k], zdev(1))
@@ -312,13 +363,15 @@
         half(1).start()
         for filler in fillers:
             filler()
-        send_across()
+        start_across()
+        chain_step(0, 0)
         hub[0] = hub_total(1)
         hub[1] = hub_total(3)
-        for t in range(up_steps):
+        if up_steps > 2:
+            chain_step(1, 0)
+        send_across()
+        for t in range(2 if up_steps > 2 else 1, up_steps - 1):
             chain_step(t, 0)
-        smoothing()
-        hub[2] = hub_total(0)
         half(0).wait_recv()
         value = hub[0]
         full_s[0, :, :lanes] = (value[:, :lanes] + half_r[0].astype(F32)).astype(BF16)
@@ -329,6 +382,10 @@
         full_s[1, :, :lanes] = value[:, :lanes].astype(BF16)
         full_s[1, :, lanes:] = (value[:, lanes:] + half_r[1].astype(F32)).astype(BF16)
         full(1).start()
+        if up_steps > 1:
+            chain_step(up_steps - 1, 0)
+        smoothing()
+        hub[2] = hub_total(0)
         finish_across()
         full(0).wait_recv()
         full(1).wait_recv()
@@ -372,7 +429,7 @@
         fillers = list(fillers)
         out_full(0, 0).start()
         out_full(1, 0).start()
-        for t in range(up_steps):
+        for t in range(up_steps - 1):
             out_step(t, 0)
         out_full(0, 0).wait_recv()
         out_half(0).start()
@@ -380,18 +437,22 @@
         out_half(1).start()
         for k in (1, 3):
             out_step(0, k)
-        collect_across()
+        out_step(up_steps - 1, 0)
         for t in range(1, up_steps):
-            if fillers:
-                fillers.pop(0)()
             for k in (1, 3):
                 out_step(t, k)
-        for filler in fillers:
-            filler()
         out_half(0).wait_recv()
         out_half(1).wait_recv()
         for t in range(up_steps):
             out_step(t, 2)
+            if t == 0:
+                pass_across()
+            if t == min(1, up_steps - 1):
+                collect_across()
+            if t >= 1:
+                fillers.pop(0)()
+        for filler in fillers:
+            filler()
         for k in (0, 1, 3, 2):
             out_last(k)
 
@@ -410,9 +471,11 @@
             out_half(i).wait_send()
 
     loads[0].wait()
+    loads[1].wait()
     forward(tab_d, blk_d, part_d, 0, slots_d)
-    loads[1].wait()
-    pl.semaphore_wait(barrier, n_col - 1 + 4)
+    for load in loads[2:]:
+        load.wait()
+    pl.semaphore_wait(barrier, chips + 4)
 
     def iteration(step, carry):
         reduce_down(pieces(functools.partial(forward, tab_a, blk_a, part_a)))
@@ -460,12 +523,21 @@
     slots_a, _, rays = blocks_across.shape
     slots_d = downward_ray_blocks.shape[0]
     rows = OWNED * slices
-    tab_a = slot_tables(
-        rays_across[0, 0], owners_across[0], tiles_across[0, 0], footprint_across[0, 0], num_tiles
-    )
-    tab_d = slot_tables(
-        rays_down[0, 0], owners_down[0], tiles_down[0, 0], footprint_down[0, 0], num_tiles
-    )
+    if slots_a == slots_d and owners_across.shape == owners_down.shape:
+        tab_a, tab_d = jax.vmap(functools.partial(slot_tables, num_tiles))(
+            jnp.concatenate([rays_across[0], rays_down[0]]),
+            jnp.concatenate([owners_across, owners_down]),
+            jnp.concatenate([tiles_across[0], tiles_down[0]]),
+            jnp.concatenate([footprint_across[0], footprint_down[0]]),
+        )
+    else:
+        tab_a = slot_tables(
+            num_tiles, rays_across[0, 0], owners_across[0], tiles_across[0, 0], footprint_across[0, 0]
+        )
+        tab_d = slot_tables(
+            num_tiles, rays_down[0, 0], owners_down[0], tiles_down[0, 0], footprint_down[0, 0]
+        )
+    chips = n_col // 2
     gap = n_row // RING
     up_steps = gap // 2
     down_steps = max(gap // 2 - 1, 1)
@@ -476,16 +548,20 @@
 
     vmem = pl.BlockSpec(memory_space=pltpu.VMEM)
     smem = pl.BlockSpec(memory_space=pltpu.SMEM)
-    anywhere = pl.BlockSpec(memory_space=pl.ANY)
+    hbm = pl.BlockSpec(memory_space=pltpu.HBM)
     own_shape = jax.ShapeDtypeStruct((rows, rays), F32)
     outs = pl.pallas_call(
         functools.partial(body, n_row, n_col),
         out_shape=(jax.ShapeDtypeStruct(voxels.shape, F32), own_shape, own_shape),
-        in_specs=[smem, smem, vmem, anywhere, anywhere, vmem, vmem, vmem, vmem],
+        in_specs=[smem, smem] + [hbm] * 7,
         out_specs=(vmem, vmem, vmem),
         scratch_shapes=[
             pltpu.VMEM(blocks_across.shape, BF16),
             pltpu.VMEM(downward_ray_blocks.shape, BF16),
+            pltpu.VMEM((rows, rays), F32),
+            pltpu.VMEM((rows, rays), F32),
+            pltpu.VMEM((rows, rays), F32),
+            pltpu.VMEM((rows, rays), F32),
             pltpu.VMEM((slots_a + 1, slices, rays), F32),
             pltpu.VMEM((slots_d + 1, slices, rays), F32),
             pltpu.VMEM((slots_a + 1, slices, tile), F32),
@@ -493,8 +569,10 @@
             pltpu.VMEM(voxels.shape, F32),
             shard(n_col),
             shard(n_row),
-            shard(n_col),
-            shard(n_col),
+            shard(chips),
+            shard(chips),
+            shard(chips),
+            shard(chips),
             shard(up_steps, RING),
             shard(up_steps, RING),
             shard(down_steps, RING),
@@ -504,11 +582,15 @@
             pltpu.VMEM((2, rows, rays // 2), BF16),
             shard(2),
             shard(2),
-            dma((2,)),
-            dma((n_col,)),
-            dma((n_col,)),
-            dma((n_col,)),
-            dma((n_col,)),
+            dma((7,)),
+            dma((1,)),
+            dma((1,)),
+            dma((chips,)),
+            dma((chips,)),
+            dma((chips,)),
+            dma((chips,)),
+            dma((chips,)),
+            dma((chips,)),
             dma((up_steps, RING)),
             dma((up_steps, RING)),
             dma((down_steps, RING)),
@@ -527,7 +609,7 @@
             dma((up_steps, RING)),
         ],
         compiler_params=pltpu.CompilerParams(
-            collective_id=0, has_side_effects=True, vmem_limit_bytes=48 << 20
+            collective_id=0, has_side_effects=True, vmem_limit_bytes=67000000
         ),
         name="tomography",
     )(

time: 189 us -> 164 us (0.87)
  the two profiles are of different devices: /device:TPU:42 before, /device:TPU:2 now
where the time goes in v2:
time: 164 us
  Pallas kernels  155 us (95%)
  local copies, waits for them, and re-layouts  5.12 us (3%)
  other arithmetic  3.24 us (2%)
    pallas_call x1, Pallas kernels, shards(): pl.pallas_call(functools.partial(body, n_row, n_col), out_shape=(jax.Shap...  155 us
    unnamed x3, local copies, waits for them, and re-layouts  4.46 us

profile of v2, /device:TPU:2, one launch (start us, length us, event | category | flops | bytes accessed | tf_op | source)
XLA Modules:
  0.0 163.8 jit_solution(15862603712152298486)
XLA Ops:
  0.6 0.7 pad_add_fusion.2
  1.3 0.7 pad_add_fusion.3
  2.0 0.2 select_reduce_fusion.2
  2.2 0.7 pad_add_fusion
  2.9 0.1 fusion
  3.0 0.2 convert_reduce_fusion.1
  3.2 0.2 convert_reduce_fusion
  3.4 0.2 select_reduce_fusion.1
  3.7 0.1 select_reduce_fusion
  3.8 0.1 slice_compare_fusion
  3.9 0.1 pad_convert_fusion
  4.0 0.6 slice_bitcast_fusion
  4.6 154.7 %tomography.1 = (f32[8,24,256]{2,1,0:T(8,128)}, f32[48,256]{1,0:T(8,128)}, f32[48,256]{1,0:T(8,128)}) custom-call(s32[8,64]{1,0:T(8,128)} %get-tuple-element.14.tab_a, s32[8,64]{1,0:T(8,128)} %get-tuple-element.13.tab_d, f32[8,24,256]{2,1,0:T(8,128)} %bitcast.44, bf16[32,256,256]{2,1,0:T(8,128)(2,1)} %blk_a_hbm.1, bf16[32,256,256]{2,1,0:T(8,128)(2,1)} %blk_d_hbm.1, ...), custom_call_target="tpu_custom_call" | custom-call | tf_op jit(solution)/shard_map/tomography/pallas_call | solution.py:553
  159.4 1.6 copy.37
  161.0 1.4 copy.38
  162.4 1.4 copy.39
  (12 shorter events, 0.1 us)

commit v3 on v2

--- a/solution.py
+++ b/solution.py
@@ -386,7 +386,6 @@
             chain_step(up_steps - 1, 0)
         smoothing()
         hub[2] = hub_total(0)
-        finish_across()
         full(0).wait_recv()
         full(1).wait_recv()
         projection = hub[2] + full_r[0].astype(F32) + full_r[1].astype(F32)
@@ -429,7 +428,9 @@
         fillers = list(fillers)
         out_full(0, 0).start()
         out_full(1, 0).start()
-        for t in range(up_steps - 1):
+        out_step(0, 0)
+        finish_across()
+        for t in range(1, up_steps - 1):
             out_step(t, 0)
         out_full(0, 0).wait_recv()
         out_half(0).start()
@@ -437,14 +438,18 @@
         out_half(1).start()
         for k in (1, 3):
             out_step(0, k)
-        out_step(up_steps - 1, 0)
-        for t in range(1, up_steps):
+        if up_steps > 1:
+            out_step(up_steps - 1, 0)
+        for t in range(1, up_steps - 1):
             for k in (1, 3):
                 out_step(t, k)
         out_half(0).wait_recv()
         out_half(1).wait_recv()
         for t in range(up_steps):
             out_step(t, 2)
+            if t == 0 and up_steps > 1:
+                for k in (1, 3):
+                    out_step(up_steps - 1, k)
             if t == 0:
                 pass_across()
             if t == min(1, up_steps - 1):
@@ -609,7 +614,7 @@
             dma((up_steps, RING)),
         ],
         compiler_params=pltpu.CompilerParams(
-            collective_id=0, has_side_effects=True, vmem_limit_bytes=67000000
+            collective_id=0, has_side_effects=True, vmem_limit_bytes=66000000
         ),
         name="tomography",
     )(

time: 164 us -> 158 us (0.963)
  the two profiles are of different devices: /device:TPU:2 before, /device:TPU:16 now
where the time goes in v3:
time: 158 us
  Pallas kernels  149 us (94%)
  local copies, waits for them, and re-layouts  5.12 us (3%)
  other arithmetic  3.24 us (2%)
    pallas_call x1, Pallas kernels, shards(): pl.pallas_call(functools.partial(body, n_row, n_col), out_shape=(jax.Shap...  149 us
    unnamed x3, local copies, waits for them, and re-layouts  4.46 us

profile of v3, /device:TPU:16, one launch (start us, length us, event | category | flops | bytes accessed | tf_op | source)
XLA Modules:
  0.0 157.6 jit_solution(11930660765045248877)
XLA Ops:
  0.6 0.7 pad_add_fusion.2
  1.3 0.7 pad_add_fusion.3
  2.0 0.2 select_reduce_fusion.2
  2.2 0.7 pad_add_fusion
  2.9 0.1 fusion
  3.0 0.2 convert_reduce_fusion.1
  3.2 0.2 convert_reduce_fusion
  3.4 0.2 select_reduce_fusion.1
  3.7 0.1 select_reduce_fusion
  3.8 0.1 slice_compare_fusion
  3.9 0.1 pad_convert_fusion
  4.0 0.6 slice_bitcast_fusion
  4.6 148.5 %tomography.1 = (f32[8,24,256]{2,1,0:T(8,128)}, f32[48,256]{1,0:T(8,128)}, f32[48,256]{1,0:T(8,128)}) custom-call(s32[8,64]{1,0:T(8,128)} %get-tuple-element.14.tab_a, s32[8,64]{1,0:T(8,128)} %get-tuple-element.13.tab_d, f32[8,24,256]{2,1,0:T(8,128)} %bitcast.44, bf16[32,256,256]{2,1,0:T(8,128)(2,1)} %blk_a_hbm.1, bf16[32,256,256]{2,1,0:T(8,128)(2,1)} %blk_d_hbm.1, ...), custom_call_target="tpu_custom_call" | custom-call | tf_op jit(solution)/shard_map/tomography/pallas_call | solution.py:558
  153.1 1.6 %copy.37 = f32[1,1,8,24,256]{4,3,2,1,0:T(8,128)} copy(f32[1,1,8,24,256]{4,3,2,1,0:T(8,128)} %bitcast.43) | data formatting | bytes 393216
  154.7 1.4 copy.38
  156.2 1.4 copy.39
  (12 shorter events, 0.1 us)
